TPU v7x, 32 devices: a whole 2x2x4 slice. The times are simulated.
32 devices in a mesh: view: 2 (over y), row: 2 (over x), col: 8 (over z, core).
Axes of the slice: x: 2, y: 2, z: 4, core: 2. Of those that a mesh axis runs over, the one named last changes fastest.
Arguments:
- inputs: bfloat16 [2, 512, 8192], P('view', 'col', 'row'), may hold values from -28 to 28, as said below
- weight: bfloat16 [8192, 8192], P('row', 'col'), may hold values from -0.0625 to 0.0625
Outputs:
- grad_hidden: bfloat16 [2, 512, 8192], P('view', 'col', 'row')
- grad_weight: float32 [8192, 8192], P('row', 'col')
Inputs may be any that keep to these rules, and one draw needn't show every extreme that they name: `inputs`: feature activations of the two views of a clip; each feature has its own scale.
All inputs are finite; a program needn't handle non-finite values.
Results may differ from a plain program's by a relative error of at most 0.025.
Values may be sent and summed in bfloat16 or wider, within the bound.
No kernel may reach another device: no remote copies, remote signals or barrier semaphores. Data moves between devices by JAX's collectives and lax.ppermute only.
A program may use at most 128 MiB of HBM per device.

v0:
```python
import math
import jax
import jax.numpy as jnp
from jax import lax
from jax.sharding import PartitionSpec as P

off_weight = 0.0051
norm_eps = 1e-05


def from_partner(block, axis, distance):
    count = lax.axis_size(axis)
    route = []
    for low in range(count):
        high = low | 1 << distance
        if high != low and high < count:
            route += [(low, high), (high, low)]
    return lax.ppermute(block, axis, route)


def shards(inputs, weight):
    hidden = lax.all_gather(inputs[0], "col", axis=0, tiled=True)
    batch = hidden.shape[0]
    columns = weight
    pre = lax.psum_scatter(
        lax.dot_general(
            columns, hidden, (((0,), (1,)), ((), ())), preferred_element_type=jnp.float32
        ).astype(jnp.bfloat16),
        "row",
        scatter_dimension=0,
        tiled=True,
    ).astype(jnp.float32)
    centred = pre - jnp.mean(pre, axis=1, keepdims=True)
    rstd = lax.rsqrt(jnp.mean(centred * centred, axis=1, keepdims=True) + norm_eps)
    own = (centred * rstd).astype(jnp.bfloat16)
    partner = from_partner(own, "view", 0)
    own_f = own.astype(jnp.float32)
    partner_f = partner.astype(jnp.float32)
    diag = jnp.sum(own_f * partner_f, axis=1, keepdims=True) / batch
    piece = lax.all_gather(partner, ("row", "col"), axis=0, tiled=True)
    corr = (
        lax.dot_general(own, piece, (((1,), (1,)), ((), ())), preferred_element_type=jnp.float32)
        / batch
    )
    mixed = jnp.dot(corr.astype(jnp.bfloat16), piece, preferred_element_type=jnp.float32)
    scale_diag = 2.0 * (diag - 1.0) - 2.0 * off_weight * diag
    dnorm = 2.0 * off_weight * mixed + scale_diag * partner_f
    inner = jnp.mean(dnorm * own_f, axis=1, keepdims=True)
    dpre = (rstd * (dnorm - jnp.mean(dnorm, axis=1, keepdims=True) - own_f * inner)).astype(
        jnp.bfloat16
    )
    grads = lax.all_gather(dpre, "row", axis=0, tiled=True)
    local_weight = lax.dot_general(
        hidden, grads, (((0,), (1,)), ((), ())), preferred_element_type=jnp.float32
    )
    grad_weight = lax.psum(local_weight.astype(jnp.bfloat16), "view").astype(
        jnp.float32
    ) / math.sqrt(2.0 * batch)
    columns = grads
    grad_hidden = lax.psum_scatter(
        lax.dot_general(
            columns, weight, (((0,), (1,)), ((), ())), preferred_element_type=jnp.float32
        ).astype(jnp.bfloat16),
        "col",
        scatter_dimension=0,
        tiled=True,
    )
    return (grad_hidden[None], grad_weight)


def solution(mesh):
    return jax.shard_map(
        shards,
        mesh=mesh,
        in_specs=(P("view", "col", "row"), P("row", "col")),
        out_specs=(P("view", "col", "row"), P("row", "col")),
        check_vma=False,
    )
```

profile of v0, /device:TPU:0, one launch (start us, length us, event | category | flops | bytes accessed | tf_op | source)
XLA Modules:
  0.0 486.3 jit_solution(11138176716313369393)
XLA Ops:
  7.2 0.0 all-gather.9.cloned.1.call-start
  7.2 0.7 all-gather.9.cloned.1.call-update
  7.9 0.0 reduce-scatter.3.cloned.1.call-start
  7.9 51.2 %all-gather.9.cloned.1.call-done = bf16[1,512,4096]{2,1,0:T(8,128)(2,1)} async-done(((bf16[1,64,4096]{2,1,0:T(8,128)(2,1)}), bf16[1,512,4096]{2,1,0:T(8,128)(2,1)}) %all-gather.9.cloned.1.call-update) | async-done | bytes 4194320 | tf_op jit(solution)/shard_map/all_gather | solution.py:22
  59.2 10.1 %fusion.4 = bf16[1024,512]{1,0:T(8,128)(2,1)} fusion(bf16[4096,1024]{1,0:T(8,128)(2,1)} %param.3, bf16[1,512,4096]{2,1,0:T(8,128)(2,1)} %all-gather.9.cloned.1.call-done), kind=kOutput, calls=%fused_computation.11 | convolution fusion | flops 4295491584 | bytes 13631488 | tf_op jit(solution)/shard_map/dot_general | solution.py:26
  69.3 0.0 reduce-scatter.3.cloned.1.call-update
  69.3 0.0 all-gather.5.cloned.1.call-start
  69.4 19.3 %reduce-scatter.3.cloned.1.call-done = bf16[512,512]{1,0:T(8,128)(2,1)} async-done(((bf16[1024,512]{1,0:T(8,128)(2,1)}), bf16[512,512]{1,0:T(8,128)(2,1)}) %reduce-scatter.3.cloned.1.call-update) | async-done | bytes 524304 | tf_op jit(solution)/shard_map/reduce_scatter | solution.py:25
  88.7 1.2 convert_reduce_fusion
  89.9 1.3 fusion.11
  91.2 1.3 fusion.12
  92.5 1.5 collective-permute-start
  94.0 12.0 %collective-permute-done = bf16[512,512]{1,0:T(8,128)(2,1)S(1)} collective-permute-done((bf16[512,512]{1,0:T(8,128)(2,1)S(1)}, bf16[512,512]{1,0:T(8,128)(2,1)S(1)}, u32[]{:S(2)}, u32[]{:S(2)}) %collective-permute-start) | collective-permute-done | bytes 524320 | tf_op jit(solution)/shard_map/ppermute | solution.py:18
  106.0 0.8 copy-done.1
  106.8 0.0 all-gather.5.cloned.1.call-update
  106.8 0.0 all-gather.7.cloned.1.call-start
  106.9 1.6 fusion.13
  108.6 72.7 %all-gather.5.cloned.1.call-done = bf16[8192,512]{1,0:T(8,128)(2,1)} async-done(((bf16[512,512]{1,0:T(8,128)(2,1)}), bf16[8192,512]{1,0:T(8,128)(2,1)}) %all-gather.5.cloned.1.call-update) | async-done | bytes 8388624 | tf_op jit(solution)/shard_map/all_gather | solution.py:40
  181.3 15.2 %fusion.19 = (f32[512]{0:T(512)S(1)}, f32[512]{0:T(512)S(1)}, f32[512,512]{1,0:T(8,128)S(1)}) fusion(bf16[512,512]{1,0:T(8,128)(2,1)S(1)} %fusion.12, bf16[512,512]{1,0:T(8,128)(2,1)} %copy-done.1, f32[512]{0:T(512)S(1)} %multiply_subtract_fusion, bf16[8192,512]{1,0:T(8,128)(2,1)} %all-gather.5.cloned.1.call-done), kind=kOutput, calls=%fused_computation.32 | convolution fusion | flops 8600420352 | bytes 10491904 | tf_op jit(solution)/shard_map/dot_general | solution.py:45
  196.6 1.1 fusion.17
  197.7 0.2 all-reduce.2.cloned.1.call-start
  197.9 19.8 %all-gather.7.cloned.1.call-done = bf16[1024,512]{1,0:T(8,128)(2,1)} async-done(((bf16[512,512]{1,0:T(8,128)(2,1)}), bf16[1024,512]{1,0:T(8,128)(2,1)}) %all-gather.7.cloned.1.call-update) | async-done | bytes 1048592 | tf_op jit(solution)/shard_map/all_gather | solution.py:52
  217.7 10.4 %convert_bitcast_fusion = bf16[4096,1024]{0,1:T(8,128)(2,1)} fusion(bf16[1024,512]{1,0:T(8,128)(2,1)} %all-gather.7.cloned.1.call-done, bf16[1,512,4096]{2,1,0:T(8,128)(2,1)} %all-gather.9.cloned.1.call-done), kind=kOutput, calls=%fused_computation.2 | convolution fusion | flops 4299161600 | bytes 13631488 | tf_op jit(solution)/shard_map/dot_general | solution.py:53
  228.2 0.0 all-reduce.2.cloned.1.call-update
  228.2 0.0 reduce-scatter.5.cloned.1.call-start
  228.2 1.1 copy-done.2
  229.4 9.6 %convolution_convert_fusion = bf16[512,4096]{1,0:T(8,128)(2,1)} fusion(bf16[1024,512]{1,0:T(8,128)(2,1)S(1)} %copy-done.2, bf16[4096,1024]{1,0:T(8,128)(2,1)} %param.3), kind=kOutput, calls=%fused_computation.3 | convolution fusion | flops 4297064448 | bytes 13631488 | tf_op jit(solution)/shard_map/dot_general | solution.py:61
  239.0 0.0 reduce-scatter.5.cloned.1.call-update
  239.0 187.4 %all-reduce.2.cloned.1.call-done = bf16[4096,1024]{0,1:T(8,128)(2,1)} async-done(((bf16[4096,1024]{0,1:T(8,128)(2,1)}), bf16[4096,1024]{0,1:T(8,128)(2,1)}) %all-reduce.2.cloned.1.call-update) | async-done | bytes 8388624 | tf_op jit(solution)/shard_map/psum | solution.py:56
  426.4 11.7 %convert_multiply_fusion = f32[4096,1024]{0,1:T(8,128)} fusion(bf16[4096,1024]{0,1:T(8,128)(2,1)} %all-reduce.2.cloned.1.call-done), kind=kLoop, calls=%fused_computation | loop fusion | flops 8388608 | bytes 25165824 | tf_op jit(solution)/shard_map/div | solution.py:56
  438.1 17.5 %copy.5 = f32[4096,1024]{1,0:T(8,128)} copy(f32[4096,1024]{0,1:T(8,128)} %convert_multiply_fusion) | data formatting | bytes 33554432
  455.6 23.8 %reduce-scatter.5.cloned.1.call-done = bf16[64,4096]{1,0:T(8,128)(2,1)} async-done(((bf16[512,4096]{1,0:T(8,128)(2,1)}), bf16[64,4096]{1,0:T(8,128)(2,1)}) %reduce-scatter.5.cloned.1.call-update) | async-done | bytes 524304 | tf_op jit(solution)/shard_map/reduce_scatter | solution.py:60
  (9 shorter events, 0.0 us)
Async XLA Ops:
  7.2 52.0 %all-gather.9.cloned.1.call-start = ((), (), s32[]{:S(2)}) async-start(), calls=%async_computation.7 | async-start | bytes 4718592 | tf_op jit(solution)/shard_map/all_gather | solution.py:22
  7.9 80.8 %reduce-scatter.3.cloned.1.call-start = ((), (), s32[]{:S(2)}) async-start(), calls=%async_computation.2 | async-start | bytes 1572864 | tf_op jit(solution)/shard_map/reduce_scatter | solution.py:25
  69.3 112.0 %all-gather.5.cloned.1.call-start = ((), (), s32[]{:S(2)}) async-start(), calls=%async_computation.3 | async-start | bytes 8912896 | tf_op jit(solution)/shard_map/all_gather | solution.py:40
  92.5 13.6 %collective-permute-start = (bf16[512,512]{1,0:T(8,128)(2,1)S(1)}, bf16[512,512]{1,0:T(8,128)(2,1)S(1)}, u32[]{:S(2)}, u32[]{:S(2)}) collective-permute-start(bf16[512,512]{1,0:T(8,128)(2,1)S(1)} %fusion.12), channel_id=1, source_target_pairs={{0,16},{16,0},{1,17},{17,1},{2,18},{18,2},{3,19},{19,3},{4,20},{20... | collective-permute-start | bytes 1572872 | tf_op jit(solution)/shard_map/ppermute | solution.py:18
  106.0 0.8 copy-start.1
  106.8 110.9 %all-gather.7.cloned.1.call-start = ((), (), s32[]{:S(2)}) async-start(), calls=%async_computation.4 | async-start | bytes 1572864 | tf_op jit(solution)/shard_map/all_gather | solution.py:52
  108.5 88.0 %copy-start = (bf16[512,512]{1,0:T(8,128)(2,1)S(1)}, bf16[512,512]{1,0:T(8,128)(2,1)}, u32[]{:S(2)}) copy-start(bf16[512,512]{1,0:T(8,128)(2,1)} %reduce-scatter.3.cloned.1.call-done) | copy-start | bytes 1572868
  197.7 228.7 %all-reduce.2.cloned.1.call-start = ((), (), s32[]{:S(2)}) async-start(), calls=%async_computation.6 | async-start | bytes 16777216 | tf_op jit(solution)/shard_map/psum | solution.py:56
  228.2 1.2 copy-start.2
  228.2 251.2 %reduce-scatter.5.cloned.1.call-start = ((), (), s32[]{:S(2)}) async-start(), calls=%async_computation.5 | async-start | bytes 4718592 | tf_op jit(solution)/shard_map/reduce_scatter | solution.py:60
Sparse Core Ops, SparseCore 0:
  9.6 49.5 all-gather.8
  69.4 19.1 reduce-scatter.2
  107.0 74.2 all-gather.4
  197.8 19.8 all-gather.6
  228.3 198.0 all-reduce.1
  429.1 50.2 reduce-scatter.4
where the time goes:
time: 487 us; the launch traced here: 486 us
  waiting for transfers between devices  387 us (79%)
  matrix products  45.4 us (9%)
  local copies, waits for them, and re-layouts  19.5 us (4%)
  other arithmetic  18.3 us (4%)
  between operations  14.2 us (3%)
    psum x1, waiting for transfers between devices, shards(): lax.psum(local_weight.astype(jnp.bfloat16), 'view').astype(jnp.float32)  187 us
    all_gather x1, waiting for transfers between devices, shards(): piece = lax.all_gather(partner, ('row', 'col'), axis=0, tiled=True)  72.7 us
    all_gather x1, waiting for transfers between devices, shards(): hidden = lax.all_gather(inputs[0], 'col', axis=0, tiled=True)  51.2 us
    reduce_scatter x1, waiting for transfers between devices, shards(): lax.psum_scatter(lax.dot_general(columns, weight, (((0,), (1,)), ((), ())...  23.8 us
    all_gather x1, waiting for transfers between devices, shards(): grads = lax.all_gather(dpre, 'row', axis=0, tiled=True)  19.8 us
    unnamed x7, local copies, waits for them, and re-layouts  19.5 us
    reduce_scatter x1, waiting for transfers between devices, shards(): lax.psum_scatter(lax.dot_general(columns, hidden, (((0,), (1,)), ((), ())...  19.3 us
    dot_general x1, matrix products, shards(): jnp.dot(corr.astype(jnp.bfloat16), piece, preferred_element_type=jnp.floa...  15.2 us
  transfers between devices with their start and end apart: 7, of which 7 were waited for; matrix products, arithmetic and copies ran while one was open for 8% of the time, Pallas kernels for 0%

commit v1 on v0

--- a/solution.py
+++ b/solution.py
@@ -6,6 +6,27 @@
 
 off_weight = 0.0051
 norm_eps = 1e-05
+
+
+def laid_out(tiles, dim):
+    shape = list(tiles.shape[1:])
+    shape[dim] *= tiles.shape[0]
+    return jnp.moveaxis(tiles, 0, dim).reshape(shape)
+
+
+def collected_by_bits(x, axis):
+    count, place = (lax.axis_size(axis), lax.axis_index(axis))
+    blocks, apart = (x[None], 1)
+    while apart < count:
+        other = lax.ppermute(blocks, axis, [(i, i ^ apart) for i in range(count)])
+        low = place & apart == 0
+        blocks = jnp.concatenate([jnp.where(low, blocks, other), jnp.where(low, other, blocks)])
+        apart *= 2
+    return blocks
+
+
+def doubled_up(x, axis, dim):
+    return laid_out(collected_by_bits(x, axis), dim)
 
 
 def from_partner(block, axis, distance):
@@ -19,7 +40,7 @@
 
 
 def shards(inputs, weight):
-    hidden = lax.all_gather(inputs[0], "col", axis=0, tiled=True)
+    hidden = doubled_up(inputs[0], "col", 0)
     batch = hidden.shape[0]
     columns = weight
     pre = lax.psum_scatter(

time: 487 us -> 567 us (1.16)
  waiting for transfers between devices: 387 us -> 474 us
  local copies, waits for them, and re-layouts: 19.5 us -> 5.27 us
  starting transfers between devices: 1.96 us -> 8.44 us
  other arithmetic: 18.3 us -> 24.3 us
    ppermute x0 -> x3, waiting for transfers between devices: none -> 116 us  [collected_by_bits(): other = lax.ppermute(blocks, axis, [(i, i ^ apart) for i in range(count)])]
    all_gather x1 -> x0, waiting for transfers between devices: 51.2 us -> none  [shards(): hidden = lax.all_gather(inputs[0], 'col', axis=0, tiled=True)]
    reduce_scatter x1, waiting for transfers between devices: 23.8 us -> 41.1 us  [shards(): lax.psum_scatter(lax.dot_general(columns, weight, (((0,), (1,)), ((), ())...]
    unnamed x7 -> x12, local copies, waits for them, and re-layouts: 19.5 us -> 5.27 us
    ppermute x0 -> x3, starting transfers between devices: none -> 6.31 us  [collected_by_bits(): other = lax.ppermute(blocks, axis, [(i, i ^ apart) for i in range(count)])]
  transfers between devices with their start and end apart: 7 -> 9, of which waited for: 7 -> 9; matrix products, arithmetic and copies ran while one was open for 8% -> 4% of each run, Pallas kernels for 0% -> 0%
where the time goes in v1:
time: 567 us; the launch traced here: 566 us
  waiting for transfers between devices  474 us (84%)
  matrix products  40.5 us (7%)
  other arithmetic  24.3 us (4%)
  between operations  13.9 us (2%)
  starting transfers between devices  8.44 us (1%)
    psum x1, waiting for transfers between devices, shards(): lax.psum(local_weight.astype(jnp.bfloat16), 'view').astype(jnp.float32)  188 us
    ppermute x3, waiting for transfers between devices, collected_by_bits(): other = lax.ppermute(blocks, axis, [(i, i ^ apart) for i in range(count)])  116 us
    all_gather x1, waiting for transfers between devices, shards(): piece = lax.all_gather(partner, ('row', 'col'), axis=0, tiled=True)  76.2 us
    reduce_scatter x1, waiting for transfers between devices, shards(): lax.psum_scatter(lax.dot_general(columns, weight, (((0,), (1,)), ((), ())...  41.1 us
    reduce_scatter x1, waiting for transfers between devices, shards(): lax.psum_scatter(lax.dot_general(columns, hidden, (((0,), (1,)), ((), ())...  21.5 us
    all_gather x1, waiting for transfers between devices, shards(): grads = lax.all_gather(dpre, 'row', axis=0, tiled=True)  19.3 us
    dot_general x1, matrix products, shards(): jnp.dot(corr.astype(jnp.bfloat16), piece, preferred_element_type=jnp.floa...  15.1 us
    ppermute x1, waiting for transfers between devices, from_partner(): return lax.ppermute(block, axis, route)  12 us
  transfers between devices with their start and end apart: 9, of which 9 were waited for; matrix products, arithmetic and copies ran while one was open for 4% of the time, Pallas kernels for 0%

profile of v1, /device:TPU:0, one launch (start us, length us, event | category | flops | bytes accessed | tf_op | source)
XLA Modules:
  0.0 566.0 jit_solution(10785361336335381510)
XLA Ops:
  7.2 0.6 collective-permute-start
  7.8 1.7 collective-permute-done
  9.5 1.1 broadcast_select_fusion.5
  10.7 3.0 collective-permute-start.1
  13.7 23.6 %collective-permute-done.1 = bf16[2,64,4096]{2,1,0:T(8,128)(2,1)} collective-permute-done((bf16[2,64,4096]{2,1,0:T(8,128)(2,1)S(1)}, bf16[2,64,4096]{2,1,0:T(8,128)(2,1)}, u32[]{:S(2)}, u32[]{:S(2)}) %collective-permute-start.1) | collective-permute-done | bytes 1048608 | tf_op jit(solution)/shard_map/ppermute | solution.py:21
  37.3 1.4 broadcast_select_fusion.3
  38.7 1.5 pad_maximum_fusion.1
  40.2 2.8 collective-permute-start.2
  42.9 90.5 %collective-permute-done.2 = bf16[4,64,4096]{2,1,0:T(8,128)(2,1)} collective-permute-done((bf16[4,64,4096]{2,1,0:T(8,128)(2,1)}, bf16[4,64,4096]{2,1,0:T(8,128)(2,1)}, u32[]{:S(2)}, u32[]{:S(2)}) %collective-permute-start.2) | collective-permute-done | bytes 2097184 | tf_op jit(solution)/shard_map/ppermute | solution.py:21
  133.4 1.9 broadcast_select_fusion.1
  135.3 0.4 pad_maximum_fusion
  135.7 2.1 copy-done.1
  137.8 1.2 slice-done.1
  139.0 5.5 fusion.2
  144.5 21.5 %reduce-scatter.3.cloned.1.call-done = bf16[512,512]{0,1:T(8,128)(2,1)} async-done(((bf16[1024,512]{0,1:T(8,128)(2,1)}), bf16[512,512]{0,1:T(8,128)(2,1)}) %reduce-scatter.3.cloned.1.call-update) | async-done | bytes 524304 | tf_op jit(solution)/shard_map/reduce_scatter | solution.py:46
  166.1 1.2 convert_reduce_fusion
  167.2 1.2 fusion.6
  168.4 1.2 fusion.7
  169.6 1.5 collective-permute-start.3
  171.1 12.0 %collective-permute-done.3 = bf16[512,512]{0,1:T(8,128)(2,1)S(1)} collective-permute-done((bf16[512,512]{0,1:T(8,128)(2,1)S(1)}, bf16[512,512]{0,1:T(8,128)(2,1)S(1)}, u32[]{:S(2)}, u32[]{:S(2)}) %collective-permute-start.3) | collective-permute-done | bytes 524320 | tf_op jit(solution)/shard_map/ppermute | solution.py:39
  183.2 0.8 copy-done.2
  184.2 1.4 fusion.8
  185.6 76.2 %all-gather.3.cloned.1.call-done = bf16[8192,512]{0,1:T(8,128)(2,1)} async-done(((bf16[512,512]{0,1:T(8,128)(2,1)}), bf16[8192,512]{0,1:T(8,128)(2,1)}) %all-gather.3.cloned.1.call-update) | async-done | bytes 8388624 | tf_op jit(solution)/shard_map/all_gather | solution.py:61
  261.8 15.1 %fusion.14 = (f32[512]{0:T(512)S(1)}, f32[512]{0:T(512)S(1)}, f32[512,512]{0,1:T(8,128)S(1)}) fusion(bf16[512,512]{0,1:T(8,128)(2,1)S(1)} %fusion.7, bf16[512,512]{0,1:T(8,128)(2,1)} %copy-done.2, f32[512]{0:T(512)S(1)} %multiply_subtract_fusion, bf16[8192,512]{0,1:T(8,128)(2,1)} %all-gather.3.cloned.1.call-done), kind=kOutput, calls=%fused_computation.39 | convolution fusion | flops 8600420352 | bytes 10491904 | tf_op jit(solution)/shard_map/dot_general | solution.py:66
  277.0 1.1 fusion.12
  278.4 19.3 %all-gather.5.cloned.1.call-done = bf16[1024,512]{0,1:T(8,128)(2,1)} async-done(((bf16[512,512]{0,1:T(8,128)(2,1)}), bf16[1024,512]{0,1:T(8,128)(2,1)}) %all-gather.5.cloned.1.call-update) | async-done | bytes 1048592 | tf_op jit(solution)/shard_map/all_gather | solution.py:73
  297.7 10.5 %convolution_convert_fusion = bf16[4096,1024]{1,0:T(8,128)(2,1)} fusion(bf16[512,4096]{1,0:T(8,128)(2,1)} %bitcast.14, bf16[1024,512]{0,1:T(8,128)(2,1)} %all-gather.5.cloned.1.call-done), kind=kOutput, calls=%fused_computation.2 | convolution fusion | flops 4299161600 | bytes 13631488 | tf_op jit(solution)/shard_map/dot_general | solution.py:74
  308.2 1.1 copy-done.3
  309.4 9.5 %convolution_convert_fusion.1 = bf16[512,4096]{1,0:T(8,128)(2,1)} fusion(bf16[1024,512]{0,1:T(8,128)(2,1)S(1)} %copy-done.3, bf16[4096,1024]{1,0:T(8,128)(2,1)} %param.3), kind=kOutput, calls=%fused_computation.3 | convolution fusion | flops 4297064448 | bytes 13631488 | tf_op jit(solution)/shard_map/dot_general | solution.py:82
  318.9 187.5 %all-reduce.2.cloned.1.call-done = bf16[4096,1024]{1,0:T(8,128)(2,1)} async-done(((bf16[4096,1024]{1,0:T(8,128)(2,1)}), bf16[4096,1024]{1,0:T(8,128)(2,1)}) %all-reduce.2.cloned.1.call-update) | async-done | bytes 8388624 | tf_op jit(solution)/shard_map/psum | solution.py:77
  506.4 12.0 %convert_multiply_fusion = f32[4096,1024]{1,0:T(8,128)} fusion(bf16[4096,1024]{1,0:T(8,128)(2,1)} %all-reduce.2.cloned.1.call-done), kind=kLoop, calls=%fused_computation | loop fusion | flops 8388608 | bytes 25165824 | tf_op jit(solution)/shard_map/div | solution.py:77
  518.4 41.1 %reduce-scatter.5.cloned.1.call-done = bf16[64,4096]{1,0:T(8,128)(2,1)} async-done(((bf16[512,4096]{1,0:T(8,128)(2,1)}), bf16[64,4096]{1,0:T(8,128)(2,1)}) %reduce-scatter.5.cloned.1.call-update) | async-done | bytes 524304 | tf_op jit(solution)/shard_map/reduce_scatter | solution.py:81
  (24 shorter events, 0.8 us)
Async XLA Ops:
  7.2 158.9 %reduce-scatter.3.cloned.1.call-start = ((), (), s32[]{:S(2)}) async-start(), calls=%async_computation.2 | async-start | bytes 1572864 | tf_op jit(solution)/shard_map/reduce_scatter | solution.py:46
  7.2 2.3 collective-permute-start
  10.7 26.6 %collective-permute-start.1 = (bf16[2,64,4096]{2,1,0:T(8,128)(2,1)S(1)}, bf16[2,64,4096]{2,1,0:T(8,128)(2,1)}, u32[]{:S(2)}, u32[]{:S(2)}) collective-permute-start(bf16[2,64,4096]{2,1,0:T(8,128)(2,1)S(1)} %pad_maximum_fusion.2), channel_id=1, source_target_pairs={{0,2},{1,3},{2,0},{3,1},{4,6},{5,7},{6,4},{7,5},{8,10},{9,11},{10,... | collective-permute-start | bytes 3145736 | tf_op jit(solution)/shard_map/ppermute | solution.py:21
  40.2 93.3 %collective-permute-start.2 = (bf16[4,64,4096]{2,1,0:T(8,128)(2,1)}, bf16[4,64,4096]{2,1,0:T(8,128)(2,1)}, u32[]{:S(2)}, u32[]{:S(2)}) collective-permute-start(bf16[4,64,4096]{2,1,0:T(8,128)(2,1)} %pad_maximum_fusion.1), channel_id=1, source_target_pairs={{0,4},{1,5},{2,6},{3,7},{4,0},{5,1},{6,2},{7,3},{8,12},{9,13},{10,... | collective-permute-start | bytes 6291464 | tf_op jit(solution)/shard_map/ppermute | solution.py:21
  42.9 94.9 %slice-start = ((s8[8388608]{0:T(1024)(128)(4,1)}), s8[4194304]{0:T(1024)(128)(4,1)S(1)}, s32[]{:S(2)}) async-start(s8[8388608]{0:T(1024)(128)(4,1)} %bitcast.15), calls=%async_computation.7 | async-start | bytes 8388608
  135.3 3.7 slice-start.1
  135.7 2.1 copy-start.1
  144.5 117.4 %all-gather.3.cloned.1.call-start = ((), (), s32[]{:S(2)}) async-start(), calls=%async_computation.3 | async-start | bytes 8912896 | tf_op jit(solution)/shard_map/all_gather | solution.py:61
  169.6 13.5 %collective-permute-start.3 = (bf16[512,512]{0,1:T(8,128)(2,1)S(1)}, bf16[512,512]{0,1:T(8,128)(2,1)S(1)}, u32[]{:S(2)}, u32[]{:S(2)}) collective-permute-start(bf16[512,512]{0,1:T(8,128)(2,1)S(1)} %fusion.7), channel_id=1, source_target_pairs={{0,16},{16,0},{1,17},{17,1},{2,18},{18,2},{3,19},{19,3},{4,20},{20... | collective-permute-start | bytes 1572872 | tf_op jit(solution)/shard_map/ppermute | solution.py:39
  183.2 0.8 copy-start.2
  184.0 113.7 %all-gather.5.cloned.1.call-start = ((), (), s32[]{:S(2)}) async-start(), calls=%async_computation.4 | async-start | bytes 1572864 | tf_op jit(solution)/shard_map/all_gather | solution.py:73
  185.6 91.4 %copy-start = (bf16[512,512]{0,1:T(8,128)(2,1)S(1)}, bf16[512,512]{0,1:T(8,128)(2,1)}, u32[]{:S(2)}) copy-start(bf16[512,512]{0,1:T(8,128)(2,1)} %reduce-scatter.3.cloned.1.call-done) | copy-start | bytes 1572868
  278.1 228.3 %all-reduce.2.cloned.1.call-start = ((), (), s32[]{:S(2)}) async-start(), calls=%async_computation.6 | async-start | bytes 16777216 | tf_op jit(solution)/shard_map/psum | solution.py:77
  308.2 1.2 copy-start.3
  308.2 251.2 %reduce-scatter.5.cloned.1.call-start = ((), (), s32[]{:S(2)}) async-start(), calls=%async_computation.5 | async-start | bytes 4718592 | tf_op jit(solution)/shard_map/reduce_scatter | solution.py:81
Sparse Core Ops, SparseCore 0:
  144.6 21.4 reduce-scatter.2
  184.1 77.7 all-gather.2
  278.2 19.4 all-gather.4
  308.3 198.0 all-reduce.1
  509.1 50.2 reduce-scatter.4
